TPU v7x, 512 devices: a whole 4x8x8 slice. The times are simulated.
512 devices in a mesh: lat: 32 (over x, z_hi, core), lev: 16 (over z_lo, y).
Axes of the slice: x: 4, y: 8, z: 8 (z_hi: 4, z_lo: 2; z = z_hi * 2 + z_lo), core: 2. Of those that a mesh axis runs over, the one named last changes fastest.
Arguments:
- thickness: float32 [64, 1024, 1152], P('lev', 'lat'), may hold values from 0.5 to 1.5
- tracer_mass: float32 [64, 1024, 1152], P('lev', 'lat'), may hold values from -6 to 6
- courant_lon: float32 [64, 1024, 1152], P('lev', 'lat'), may hold values from -0.12 to 0.12
- courant_lat: float32 [64, 1024, 1152], P('lev', 'lat'), may hold values from -0.12 to 0.12
- filter_cut: int32 [1024], P('lat'), may hold values from 4 to 576, as said below
- target_weights: int32 [64, 1024, 1152], P(None, 'lat', 'lev'), may hold values from 1 to 8
Outputs:
- remapped_thickness: float32 [64, 1024, 1152], P(None, 'lat', 'lev')
- remapped_tracer: float32 [64, 1024, 1152], P(None, 'lat', 'lev')
Inputs may be any that keep to these rules, and one draw needn't show every extreme that they name: filter_cut is 576 on every row outside the first 64 and the last 64 latitude rows; inside them it is at least 4.
All inputs are finite; a program needn't handle non-finite values.
Results may differ from a plain program's by a relative error of at most 0.0003.
Values sent between devices are 32-bit elements; how exact they have to be, the bound alone decides.
A program may use at most 64 MiB of HBM per device.

v0:
```python
import functools

import jax
import jax.numpy as jnp
import ml_dtypes
import numpy as np
from jax import lax
from jax.experimental import pallas as pl
from jax.experimental.pallas import tpu as pltpu
from jax.sharding import PartitionSpec as P

ITERS = 2
LANES = 128
MESH = pl.DeviceIdType.MESH


def split_bf16(table):
    high = table.astype(ml_dtypes.bfloat16)
    low = (table - high.astype(np.float64)).astype(ml_dtypes.bfloat16)
    return high, low


def fourier_tables(lon):
    half = lon // 2
    quarter = half // 2
    index = np.arange(half)
    even_wave = np.where(index <= quarter, 2 * index, 2 * (index - quarter))
    even_sine = index > quarter
    odd_wave = np.where(index < quarter, 2 * index + 1, 2 * (index - quarter) + 1)
    odd_sine = index >= quarter
    parts = []
    inverse = []
    for wave, sine in ((even_wave, even_sine), (odd_wave, odd_sine)):
        phase = 2.0 * np.pi / lon * (wave[:, None] * index[None, :] % lon)
        basis = np.where(sine[:, None], np.sin(phase), np.cos(phase))
        scale = np.where((wave == 0) | (wave == half), 1.0 / lon, 2.0 / lon)
        parts.append(basis)
        inverse.append((basis * scale[:, None]).T)
    forward_high, forward_low = split_bf16(np.stack(parts))
    inverse_high, inverse_low = split_bf16(np.stack(inverse))
    return np.stack([forward_high, forward_low, inverse_high, inverse_low])


def face_cosine(row, lat_total):
    return jnp.sin(jnp.pi / lat_total * jnp.minimum(row + 1, lat_total - row - 1).astype(jnp.float32))


def cell_cosine(row, lat_total):
    return jnp.sin(jnp.pi / lat_total * (row.astype(jnp.float32) + 0.5))


def advance(field, north, south_flux, lon_pos, lon_neg, lat_pos, lat_neg, inv_cos):
    width = field.shape[1]
    east = pltpu.roll(field, width - 1, axis=1)
    lon_flux = lon_pos * field + lon_neg * east
    lat_flux = lat_pos * field + lat_neg * north
    return field - (lon_flux - pltpu.roll(lon_flux, 1, axis=1)) - (lat_flux - south_flux(lat_flux)) * inv_cos


def by_sign(courant, scale=None):
    parts = jnp.maximum(courant, 0.0), jnp.minimum(courant, 0.0)
    return parts if scale is None else tuple(part * scale for part in parts)


def transport(lat, lat_total, arrays, pack, extra, inner_first, halo, exchange, thick_rows, tracer_rows, tend_rows):
    levels, rows, width = arrays[0].shape
    first_row = lat * rows
    for which, array in enumerate(arrays):
        for level in range(levels):
            for row in range(2):
                pack[0, which, pl.ds(row * levels + level, 1), :] = array[level, pl.ds(rows - 2 + row, 1), :]
                pack[1, which, pl.ds(row * levels + level, 1), :] = array[level, pl.ds(row, 1), :]
                extra[which, pl.ds(row * levels + level, 1), :] = array[level, pl.ds((2, rows - 3)[row], 1), :]
    finish = exchange()
    thick, tracer, lat_courant, lon_courant = arrays
    row_index = first_row + lax.broadcasted_iota(jnp.int32, (rows, 1), 0)
    cos_faces = face_cosine(row_index, lat_total)
    inv_cos = 1.0 / cell_cosine(row_index, lat_total)

    @pl.loop(0, levels)
    def _(level):
        lat_now = lat_courant[level]
        lat_pos, lat_neg = by_sign(0.5 * (lat_now + pltpu.roll(lat_now, rows - 1, axis=0)), cos_faces)
        lon_pos, lon_neg = by_sign(lon_courant[level])
        place = pl.ds(pl.multiple_of(level * rows, rows), rows)
        for which, array in enumerate((thick, tracer)):
            start = array[level]
            field = start
            for step in range(ITERS):
                field = advance(
                    field, pltpu.roll(field, rows - 1, axis=0), lambda flux: pltpu.roll(flux, 1, axis=0),
                    lon_pos, lon_neg, lat_pos, lat_neg, inv_cos,
                )
                if step == 0:
                    inner_first[which, pl.ds(level, 1), :] = field[2:3]
                    inner_first[which, pl.ds(levels + level, 1), :] = field[rows - 3 : rows - 2]
            if which == 0:
                thick_rows[place, :] = field
            else:
                tend = field - start
                tend_rows[place, :] = tend
                tracer_rows[place, :] = start + tend

    finish()
    sub = lax.broadcasted_iota(jnp.int32, (2 * levels, 1), 0)
    strip_row = jnp.where(sub < levels, first_row - 2, first_row + rows - 3)
    cos_strip = [face_cosine(strip_row + p, lat_total) for p in range(4)]
    inv_strip = [1.0 / cell_cosine(strip_row + p, lat_total) for p in range(4)]

    def strip(which):
        below, above = halo[0, which], halo[1, which]
        last, first, third = pack[0, which], pack[1, which], extra[which]
        halves = (
            (below[:levels], third[levels:]),
            (below[levels:], last[:levels]),
            (first[:levels], last[levels:]),
            (first[levels:], above[:levels]),
            (third[:levels], above[levels:]),
        )
        return [jnp.concatenate(pair, axis=0) for pair in halves]

    lat_strip = strip(2)
    lat_parts = [by_sign(0.5 * (lat_strip[p] + lat_strip[p + 1]), cos_strip[p]) for p in range(4)]
    lon_parts = [by_sign(values) for values in strip(3)]
    for which in range(2):
        start = strip(which)
        field = start
        for step in range(ITERS):
            moved = []
            flux = lat_parts[0][0] * field[0] + lat_parts[0][1] * field[1]
            for p in range(1, 4):
                before = flux
                moved.append(advance(
                    field[p], field[p + 1], lambda _: before,
                    *lon_parts[p], *lat_parts[p], inv_strip[p],
                ))
                flux = lat_parts[p][0] * field[p] + lat_parts[p][1] * field[p + 1]
            field = [inner_first[which], *moved, inner_first[which]]
        for p, side, row in ((2, 0, 0), (3, 0, 1), (1, 1, rows - 2), (2, 1, rows - 1)):
            tend = field[p] - start[p]
            done = start[p] + tend
            for level in range(levels):
                source = slice(side * levels + level, side * levels + level + 1)
                place = pl.ds(level * rows + row, 1)
                if which == 0:
                    thick_rows[place, :] = field[p][source]
                else:
                    tend_rows[place, :] = tend[source]
                    tracer_rows[place, :] = done[source]


def to_columns(source, target):
    for block in range(source.shape[1] // LANES):
        piece = pl.ds(block * LANES, LANES)
        target[piece, :] = source[:, piece].T


def add_damped(cut, tend, tables, tracer):
    half = tend.shape[0] // 2
    quarter = half // 2
    index = lax.broadcasted_iota(jnp.int32, (half, 1), 0)
    first, second = tend[pl.ds(0, half), :], tend[pl.ds(half, half), :]

    def times(stage, parity, columns):
        high = columns.astype(jnp.bfloat16)
        low = (columns - high.astype(jnp.float32)).astype(jnp.bfloat16)
        both = jnp.dot(tables[2 * stage, parity], jnp.concatenate([high, low], axis=1), preferred_element_type=jnp.float32)
        rest = jnp.dot(tables[2 * stage + 1, parity], high, preferred_element_type=jnp.float32)
        return both[:, :LANES] + (both[:, LANES:] + rest)

    changes = []
    for parity in range(2):
        if parity == 0:
            wave = jnp.where(index <= quarter, 2 * index, 2 * (index - quarter))
        else:
            wave = jnp.where(index < quarter, 2 * index + 1, 2 * (index - quarter) + 1)
        ratio = cut * (1.0 / jnp.maximum(wave, 1).astype(jnp.float32))
        damping = jnp.where(wave == 0, 1.0, jnp.minimum(1.0, ratio * ratio))
        coefficients = times(0, parity, first + second if parity == 0 else first - second)
        changes.append(times(1, parity, coefficients * (damping - 1.0)))
    tracer[pl.ds(0, half), :] += changes[0] + changes[1]
    tracer[pl.ds(half, half), :] += changes[0] - changes[1]


def prepare_weights(weights, fraction, fraction_cols):
    level_total, rows, dest = weights.shape
    levels = LANES // rows

    def add(level, total):
        total = total + weights[level]
        fraction[level, :, pl.ds(0, dest)] = total.astype(jnp.float32)
        return total

    total = lax.fori_loop(0, level_total, add, jnp.zeros((rows, dest), jnp.int32), unroll=8)
    inverse = 1.0 / total.astype(jnp.float32)

    @pl.loop(0, level_total // levels)
    def _(group):
        here = pl.ds(group * levels, levels)
        scaled = fraction[here, :, pl.ds(0, dest)] * inverse[None]
        fraction[here, :, pl.ds(0, dest)] = scaled
        fraction_cols[group] = fraction[here].reshape(LANES, LANES).T[:dest]


def interpolate(rows, piece, thick, tracer, fraction_cols, tops_turned, slopes_turned, below, mass_cols):
    sources = thick.shape[0]
    levels = LANES // rows
    groups = sources
    lane_level = lax.broadcasted_iota(jnp.int32, (8, LANES), 1) // rows
    here = pl.ds(pl.multiple_of(piece * 8, 8), 8)
    zero = jnp.zeros((8, LANES), jnp.float32)

    def turn(values, count):
        return pltpu.roll(values, count * rows, axis=1)

    carry = offset = last = zero
    for source in range(sources):
        layer = thick[source, here, :]
        ratio = tracer[source, here, :] / layer
        one = turn(layer, 1)
        two = layer + jnp.where(lane_level >= 1, one, 0.0)
        inclusive = two + jnp.where(lane_level >= 2, turn(two, 2), 0.0)
        pair = layer + one
        tops = carry + (inclusive - layer)
        carry = carry + (pair + turn(pair, 2))
        moved = turn(ratio, 1)
        slope = ratio - jnp.where(lane_level >= 1, moved, last)
        last = moved
        offset = offset + slope * tops
        for count in range(levels):
            tops_turned[source * levels + count] = turn(tops, count) if count else tops
            slopes_turned[source * levels + count] = turn(slope, count) if count else slope
    offset = offset + turn(offset, 1)
    offset = offset + turn(offset, 2)
    mass_cols[here, :] = carry
    targets = [carry * fraction_cols[group, here, :] for group in range(groups)]

    def accumulate(index, sums):
        tops, slope = tops_turned[index], slopes_turned[index]
        return tuple(s + slope * jnp.maximum(t, tops) for s, t in zip(sums, targets))

    sums = lax.fori_loop(0, sources * levels, accumulate, (zero,) * groups, unroll=4)
    for group in range(groups):
        below[group, here, :] = sums[group] - offset


def step_kernel(
    n_lat, n_lev, lat_total, chunks,
    thick_hbm, tracer_hbm, lon_hbm, lat_hbm, cut_hbm, weights_hbm, tables_hbm,
    below, fraction, mass_cols,
    thick_in, tracer_in, lon_in, lat_in, cut_in, weights_in, tables,
    pack, halo, extra, inner_first, thick_rows, tracer_rows, tend_rows, thick_send, tracer_send, tend_cols, cut_lanes,
    thick_cols, tracer_cols, fraction_cols, tops_turned, slopes_turned,
    load_sem, halo_sent, halo_got, sent, got,
):
    levels, rows, width = thick_in.shape
    dest = width // n_lev
    lat = lax.axis_index("lat")
    lev = lax.axis_index("lev")
    north = lax.rem(lat + 1, n_lat)
    south = lax.rem(lat + n_lat - 1, n_lat)
    polar = (lat < 2) | (lat >= n_lat - 2)
    barrier = pltpu.get_barrier_semaphore()
    for place in (north, south):
        pl.semaphore_signal(barrier, inc=1, device_id={"lat": place}, device_id_type=MESH)
    for offset in range(1, n_lev):
        pl.semaphore_signal(barrier, inc=1, device_id={"lev": lax.rem(lev + offset, n_lev)}, device_id_type=MESH)
    pairs = (
        (thick_hbm, thick_in), (tracer_hbm, tracer_in), (lat_hbm, lat_in), (lon_hbm, lon_in),
        (weights_hbm, weights_in), (cut_hbm, cut_in), (tables_hbm, tables),
    )
    loads = [pltpu.make_async_copy(source, target, load_sem.at[i]) for i, (source, target) in enumerate(pairs)]
    for load in loads[:6]:
        load.start()

    @pl.when(polar)
    def _():
        loads[6].start()

    for load in loads[:4]:
        load.wait()

    def exchange():
        pl.semaphore_wait(barrier, n_lev + 1)
        copies = []
        for side, place in ((0, north), (1, south)):
            copy = pltpu.make_async_remote_copy(
                src_ref=pack.at[side], dst_ref=halo.at[side], send_sem=halo_sent.at[side], recv_sem=halo_got.at[side],
                device_id={"lat": place}, device_id_type=MESH,
            )
            copy.start()
            copies.append(copy)

        def finish():
            for copy in copies:
                copy.wait()

        return finish

    transport(
        lat, lat_total, (thick_in, tracer_in, lat_in, lon_in), pack, extra, inner_first, halo, exchange,
        thick_rows, tracer_rows, tend_rows,
    )

    def send(source, target, which, first, count):
        started = []
        for offset in range(1, n_lev):
            other = lax.rem(lev + offset, n_lev)
            copy = pltpu.make_async_remote_copy(
                src_ref=source.at[pl.ds(pl.multiple_of(other * dest + first, 8), count)],
                dst_ref=target.at[lev, pl.ds(first, count)],
                send_sem=sent.at[which, offset - 1], recv_sem=got.at[which, offset - 1],
                device_id={"lev": other}, device_id_type=MESH,
            )
            copy.start()
            started.append(copy)
        return started

    to_columns(thick_rows, thick_send)
    thick_copies = send(thick_send, thick_cols, 0, 0, dest)
    to_columns(tracer_rows, tracer_send)
    for load in loads[4:6]:
        load.wait()

    @pl.when(polar)
    def _():
        to_columns(tend_rows, tend_cols)
        for level in range(levels):
            cut_lanes[:, pl.ds(level * rows, rows)] = jnp.broadcast_to(cut_in[...].astype(jnp.float32), (8, rows))
        loads[6].wait()
        add_damped(cut_lanes[pl.ds(0, 1), :], tend_cols, tables, tracer_send)

    bounds = [sum(chunks[:i]) for i in range(len(chunks) + 1)]
    tracer_copies = [
        send(tracer_send, tracer_cols, 1 + i, 8 * bounds[i], 8 * chunks[i]) for i in range(len(chunks))
    ]
    mine = pl.ds(pl.multiple_of(lev * dest, 8), dest)
    thick_cols[lev] = thick_send[mine, :]
    tracer_cols[lev] = tracer_send[mine, :]
    prepare_weights(weights_in, fraction, fraction_cols)
    for copy in thick_copies:
        copy.wait()
    for i in range(len(chunks)):
        for copy in tracer_copies[i]:
            copy.wait()

        @pl.loop(bounds[i], bounds[i + 1])
        def _(piece):
            interpolate(rows, piece, thick_cols, tracer_cols, fraction_cols, tops_turned, slopes_turned, below, mass_cols)


def finish_kernel(below, fraction, mass_cols, thick_hbm, tracer_hbm, new_thick, new_tracer, sems):
    groups = below.shape[0]
    levels, rows, dest = new_thick.shape[0] // groups, new_thick.shape[1], new_thick.shape[2]
    mass = mass_cols[...].T[:rows, :dest]
    target_before = below_before = jnp.zeros((rows, dest), jnp.float32)
    copies = []

    def put(which, group, source, target):
        place = pl.ds(group * levels, levels)
        copy = pltpu.make_async_copy(source.at[place], target.at[place], sems.at[which, group])
        copy.start()
        copies.append(copy)

    for group in range(groups):
        block = below[group].T.reshape(levels, rows, LANES)
        for inner in range(levels):
            level = group * levels + inner
            target = mass * fraction[level, :, pl.ds(0, dest)]
            new_thick[level] = target - target_before
            target_before = target
            now = block[inner, :, :dest]
            new_tracer[level] = now - below_before
            below_before = now
        put(0, group, new_thick, thick_hbm)
        put(1, group, new_tracer, tracer_hbm)
    for copy in copies:
        copy.wait()


def chunks_of(pieces):
    half = (pieces - 1) // 2
    return (pieces - 1 - half, half, 1)


def on_device(n_lat, n_lev, thickness, tracer_mass, courant_lon, courant_lat, filter_cut, target_weights):
    levels, rows, width = thickness.shape
    lat_total = n_lat * rows
    dest = width // n_lev
    level_total = target_weights.shape[0]
    groups = level_total * rows // LANES
    tables = fourier_tables(width)
    chunks = chunks_of(dest // 8)
    vmem, hbm = pl.BlockSpec(memory_space=pltpu.VMEM), pl.BlockSpec(memory_space=pltpu.HBM)
    f32, dma = jnp.float32, pltpu.SemaphoreType.DMA
    block = thickness.shape
    sums = (
        jax.ShapeDtypeStruct((groups, LANES, LANES), f32),
        jax.ShapeDtypeStruct((level_total, rows, LANES), f32),
        jax.ShapeDtypeStruct((LANES, LANES), f32),
    )
    shapes = (
        *[block] * 4, (1, rows), target_weights.shape, tables.shape,
        (2, 4, 2 * levels, width), (2, 4, 2 * levels, width), (4, 2 * levels, width), (2, 2 * levels, width),
        *[(LANES, width)] * 3, *[(width, LANES)] * 3, (8, LANES),
        (n_lev, dest, LANES), (n_lev, dest, LANES), (groups, dest, LANES), (level_total, 8, LANES), (level_total, 8, LANES),
    )
    kinds = [f32] * 4 + [jnp.int32] * 2 + [jnp.bfloat16] + [f32] * (len(shapes) - 7)
    arrays = (
        thickness, tracer_mass, courant_lon, courant_lat, filter_cut.reshape(1, rows), target_weights, jnp.asarray(tables),
    )
    columns = pl.pallas_call(
        functools.partial(step_kernel, n_lat, n_lev, lat_total, chunks),
        out_shape=sums,
        in_specs=[hbm] * 7,
        out_specs=(vmem,) * 3,
        scratch_shapes=[pltpu.VMEM(shape, kind) for shape, kind in zip(shapes, kinds)]
        + [dma((7,)), dma((2,)), dma((2,)), dma((1 + len(chunks), n_lev - 1)), dma((1 + len(chunks), n_lev - 1))],
        compiler_params=pltpu.CompilerParams(collective_id=0, has_side_effects=True, vmem_limit_bytes=48 << 20),
        name="step",
    )(*(pltpu.with_memory_space_constraint(array, pltpu.HBM) for array in arrays))
    result = jax.ShapeDtypeStruct(target_weights.shape, f32)
    return pl.pallas_call(
        finish_kernel,
        out_shape=(result, result),
        in_specs=[vmem] * 3,
        out_specs=(hbm, hbm),
        scratch_shapes=[
            pltpu.VMEM(target_weights.shape, f32), pltpu.VMEM(target_weights.shape, f32), dma((2, groups)),
        ],
        compiler_params=pltpu.CompilerParams(vmem_limit_bytes=32 << 20),
        name="finish",
    )(*columns)


def solution(mesh):
    n_lat, n_lev = mesh.shape["lat"], mesh.shape["lev"]
    placed = (
        P("lev", "lat", None),
        P("lev", "lat", None),
        P("lev", "lat", None),
        P("lev", "lat", None),
        P("lat"),
        P(None, "lat", "lev"),
    )
    return jax.shard_map(
        functools.partial(on_device, n_lat, n_lev),
        mesh=mesh,
        in_specs=placed,
        out_specs=(P(None, "lat", "lev"), P(None, "lat", "lev")),
        check_vma=False,
    )
```

profile of v0, /device:TPU:6, one launch (start us, length us, event | category | flops | bytes accessed | tf_op | source)
XLA Modules:
  0.0 52.1 jit_solution(4634254108637916285)
XLA Ops:
  0.6 49.8 %step.1 = (f32[16,128,128]{2,1,0:T(8,128)S(1)}, f32[64,32,128]{2,1,0:T(8,128)S(1)}, f32[128,128]{1,0:T(8,128)S(1)}) custom-call(f32[4,32,1152]{2,1,0:T(8,128)} %thick_hbm.1, f32[4,32,1152]{2,1,0:T(8,128)} %tracer_hbm.1, f32[4,32,1152]{2,1,0:T(8,128)} %lon_hbm.1, f32[4,32,1152]{2,1,0:T(8,128)} %lat_hbm.1, s32[1,32]{1,0:T(1,128)} %bitcast.1, ...), custom_call_target="tpu_custom_call" | custom-call | tf_op jit(solution)/shard_map/step/pallas_call | solution.py:412
  50.4 1.7 %finish.1 = (f32[64,32,72]{2,1,0:T(8,128)}, f32[64,32,72]{2,1,0:T(8,128)}) custom-call(f32[16,128,128]{2,1,0:T(8,128)S(1)} %get-tuple-element.5.below, f32[64,32,128]{2,1,0:T(8,128)S(1)} %get-tuple-element.6.fraction, f32[128,128]{1,0:T(8,128)S(1)} %get-tuple-element.7.mass_cols), custom_call_target="tpu_custom_call" | custom-call | tf_op jit(solution)/shard_map/finish/pallas_call | solution.py:423
where the time goes:
time: 52.7 us; the launch traced here: 52.1 us
  Pallas kernels  51.5 us (98%)
  between operations  0.64 us (1%)
    pallas_call x1, Pallas kernels, on_device(): pl.pallas_call(functools.partial(step_kernel, n_lat, n_lev, lat_total, ch...  49.8 us
    pallas_call x1, Pallas kernels, on_device(): pl.pallas_call(finish_kernel, out_shape=(result, result), in_specs=[vmem]...  1.68 us

commit v1 on v0

v1 whole, which is shorter than its diff:
```python
import functools

import jax
import jax.numpy as jnp
import ml_dtypes
import numpy as np
from jax import lax
from jax.experimental import pallas as pl
from jax.experimental.pallas import tpu as pltpu
from jax.sharding import PartitionSpec as P

ITERS = 2
LANES = 128
MESH = pl.DeviceIdType.MESH


def split_bf16(table):
    high = table.astype(ml_dtypes.bfloat16)
    low = (table - high.astype(np.float64)).astype(ml_dtypes.bfloat16)
    return high, low


def fourier_tables(lon):
    half = lon // 2
    quarter = half // 2
    index = np.arange(half)
    even_wave = np.where(index <= quarter, 2 * index, 2 * (index - quarter))
    even_sine = index > quarter
    odd_wave = np.where(index < quarter, 2 * index + 1, 2 * (index - quarter) + 1)
    odd_sine = index >= quarter
    parts = []
    inverse = []
    for wave, sine in ((even_wave, even_sine), (odd_wave, odd_sine)):
        phase = 2.0 * np.pi / lon * (wave[:, None] * index[None, :] % lon)
        basis = np.where(sine[:, None], np.sin(phase), np.cos(phase))
        scale = np.where((wave == 0) | (wave == half), 1.0 / lon, 2.0 / lon)
        parts.append(basis)
        inverse.append((basis * scale[:, None]).T)
    forward_high, forward_low = split_bf16(np.stack(parts))
    inverse_high, inverse_low = split_bf16(np.stack(inverse))
    return np.stack([forward_high, forward_low, inverse_high, inverse_low])


def face_cosine(row, lat_total):
    return jnp.sin(jnp.pi / lat_total * jnp.minimum(row + 1, lat_total - row - 1).astype(jnp.float32))


def cell_cosine(row, lat_total):
    return jnp.sin(jnp.pi / lat_total * (row.astype(jnp.float32) + 0.5))


def advance(field, north, south_flux, lon_pos, lon_neg, lat_pos, lat_neg, inv_cos):
    width = field.shape[1]
    east = pltpu.roll(field, width - 1, axis=1)
    lon_flux = lon_pos * field + lon_neg * east
    lat_flux = lat_pos * field + lat_neg * north
    return field - (lon_flux - pltpu.roll(lon_flux, 1, axis=1)) - (lat_flux - south_flux(lat_flux)) * inv_cos


def by_sign(courant, scale=None):
    parts = jnp.maximum(courant, 0.0), jnp.minimum(courant, 0.0)
    return parts if scale is None else tuple(part * scale for part in parts)


def spread(rows):
    return jnp.concatenate([rows[..., 8:, :], rows[..., :8, :]], axis=-2)


def lane_half(rows):
    return lax.rem(lax.broadcasted_iota(jnp.int32, (8, LANES), 1), rows) < rows // 2


def pair_up(first, second, rows):
    low = lane_half(rows)
    middle = jnp.where(low, first, pltpu.roll(second, rows // 2, axis=1))
    outer = jnp.where(low, pltpu.roll(first, LANES - rows // 2, axis=1), second)
    return middle, outer


def inner_rows(lat_total, arrays, arrive, thick_rows, tracer_rows, tend_rows, to_north, to_south, third, inner_first):
    thick, tracer, lat_courant, lon_courant = arrays
    levels, rows, width = thick.shape
    first_row = lax.axis_index("lat") * rows
    row_index = first_row + lax.broadcasted_iota(jnp.int32, (rows, 1), 0)
    cos_faces = face_cosine(row_index, lat_total)
    inv_cos = 1.0 / cell_cosine(row_index, lat_total)

    @pl.loop(0, levels)
    def _(level):
        arrive(level)
        for which, array in enumerate(arrays):
            for row in range(2):
                place = pl.ds(row * levels + level, 1)
                to_north[which, place, :] = array[level, pl.ds(rows - 2 + row, 1), :]
                to_south[which, place, :] = array[level, pl.ds(row, 1), :]
                third[which, place, :] = array[level, pl.ds((2, rows - 3)[row], 1), :]
        lat_now = lat_courant[level]
        lat_pos, lat_neg = by_sign(0.5 * (lat_now + pltpu.roll(lat_now, rows - 1, axis=0)), cos_faces)
        lon_pos, lon_neg = by_sign(lon_courant[level])
        place = pl.ds(pl.multiple_of(level * rows, rows), rows)
        for which, array in enumerate((thick, tracer)):
            start = array[level]
            field = start
            for step in range(ITERS):
                field = advance(
                    field, pltpu.roll(field, rows - 1, axis=0), lambda flux: pltpu.roll(flux, 1, axis=0),
                    lon_pos, lon_neg, lat_pos, lat_neg, inv_cos,
                )
                if step == 0:
                    inner_first[which, pl.ds(level, 1), :] = field[2:3]
                    inner_first[which, pl.ds(levels + level, 1), :] = field[rows - 3 : rows - 2]
            if which == 0:
                thick_rows[place, :] = spread(field)
            else:
                tend = field - start
                tend_rows[place, :] = spread(tend)
                tracer_rows[place, :] = spread(start + tend)


def edges(lat_total, rows, below, above, to_north, to_south, third, inner_first, thick_rows, tracer_rows, tend_rows):
    levels = below.shape[1] // 2
    first_row = lax.axis_index("lat") * rows
    sub = lax.broadcasted_iota(jnp.int32, (2 * levels, 1), 0)
    strip_row = jnp.where(sub < levels, first_row - 2, first_row + rows - 3)
    cos_strip = [face_cosine(strip_row + p, lat_total) for p in range(4)]
    inv_strip = [1.0 / cell_cosine(strip_row + p, lat_total) for p in range(4)]

    def strip(which):
        low, high, last, first, inner = (ref[which] for ref in (below, above, to_north, to_south, third))
        halves = (
            (low[:levels], inner[levels:]),
            (low[levels:], last[:levels]),
            (first[:levels], last[levels:]),
            (first[levels:], high[:levels]),
            (inner[:levels], high[levels:]),
        )
        return [jnp.concatenate(pair, axis=0) for pair in halves]

    lat_strip = strip(2)
    lat_parts = [by_sign(0.5 * (lat_strip[p] + lat_strip[p + 1]), cos_strip[p]) for p in range(4)]
    lon_parts = [by_sign(values) for values in strip(3)]
    for which in range(2):
        start = strip(which)
        field = start
        for step in range(ITERS):
            moved = []
            flux = lat_parts[0][0] * field[0] + lat_parts[0][1] * field[1]
            for p in range(1, 4):
                before = flux
                moved.append(advance(
                    field[p], field[p + 1], lambda _: before,
                    *lon_parts[p], *lat_parts[p], inv_strip[p],
                ))
                flux = lat_parts[p][0] * field[p] + lat_parts[p][1] * field[p + 1]
            field = [inner_first[which], *moved, inner_first[which]]
        for p, side, row in ((2, 0, 0), (3, 0, 1), (1, 1, rows - 2), (2, 1, rows - 1)):
            tend = field[p] - start[p]
            done = start[p] + tend
            for level in range(levels):
                source = slice(side * levels + level, side * levels + level + 1)
                place = pl.ds(level * rows + (row - 8) % rows, 1)
                if which == 0:
                    thick_rows[place, :] = field[p][source]
                else:
                    tend_rows[place, :] = tend[source]
                    tracer_rows[place, :] = done[source]


def to_columns(source, target):
    for block in range(source.shape[1] // LANES):
        piece = pl.ds(block * LANES, LANES)
        target[piece, :] = source[:, piece].T


def add_damped(cut, tend, tables, tracer):
    half = tend.shape[0] // 2
    quarter = half // 2
    index = lax.broadcasted_iota(jnp.int32, (half, 1), 0)
    first, second = tend[pl.ds(0, half), :], tend[pl.ds(half, half), :]

    def times(stage, parity, columns):
        high = columns.astype(jnp.bfloat16)
        low = (columns - high.astype(jnp.float32)).astype(jnp.bfloat16)
        both = jnp.dot(tables[2 * stage, parity], jnp.concatenate([high, low], axis=1), preferred_element_type=jnp.float32)
        rest = jnp.dot(tables[2 * stage + 1, parity], high, preferred_element_type=jnp.float32)
        return both[:, :LANES] + (both[:, LANES:] + rest)

    changes = []
    for parity in range(2):
        if parity == 0:
            wave = jnp.where(index <= quarter, 2 * index, 2 * (index - quarter))
        else:
            wave = jnp.where(index < quarter, 2 * index + 1, 2 * (index - quarter) + 1)
        ratio = cut * (1.0 / jnp.maximum(wave, 1).astype(jnp.float32))
        damping = jnp.where(wave == 0, 1.0, jnp.minimum(1.0, ratio * ratio))
        coefficients = times(0, parity, first + second if parity == 0 else first - second)
        changes.append(times(1, parity, coefficients * (damping - 1.0)))
    tracer[pl.ds(0, half), :] += changes[0] + changes[1]
    tracer[pl.ds(half, half), :] += changes[0] - changes[1]


def prepare_weights(weights, fraction, fraction_cols):
    level_total, rows, dest = weights.shape
    levels = LANES // rows
    pieces = dest // 8

    def add(level, total):
        total = total + weights[level]
        fraction[level, :, pl.ds(0, dest)] = total.astype(jnp.float32)
        return total

    total = lax.fori_loop(0, level_total, add, jnp.zeros((rows, dest), jnp.int32), unroll=8)
    inverse = 1.0 / total.astype(jnp.float32)

    @pl.loop(0, level_total // levels)
    def _(group):
        here = pl.ds(group * levels, levels)
        fraction[here, :, pl.ds(0, dest)] = fraction[here, :, pl.ds(0, dest)] * inverse[None]
        columns = spread(fraction[here]).reshape(LANES, LANES).T
        for pair in range(pieces // 2):
            middle, outer = pair_up(columns[16 * pair : 16 * pair + 8], columns[16 * pair + 8 : 16 * pair + 16], rows)
            fraction_cols[group, pl.ds(8 * pair, 8), :] = middle
            fraction_cols[group, pl.ds(8 * (pieces // 2 + pair), 8), :] = outer
        if pieces % 2:
            fraction_cols[group, pl.ds(dest - 8, 8), :] = columns[dest - 8 : dest]


def interpolate(rows, piece, place, thick, tracer, fraction_cols, tops_turned, slopes_turned, below, mass_cols):
    sources = thick.shape[0]
    levels = LANES // rows
    groups = sources
    lane_level = lax.broadcasted_iota(jnp.int32, (8, LANES), 1) // rows
    there = pl.ds(pl.multiple_of(piece * 8, 8), 8)
    here = pl.ds(pl.multiple_of(place * 8, 8), 8)
    zero = jnp.zeros((8, LANES), jnp.float32)

    def turn(values, count):
        return pltpu.roll(values, count * rows, axis=1)

    carry = offset = last = zero
    for source in range(sources):
        layer = thick[source, there, :]
        ratio = tracer[source, there, :] / layer
        one = turn(layer, 1)
        two = layer + jnp.where(lane_level >= 1, one, 0.0)
        inclusive = two + jnp.where(lane_level >= 2, turn(two, 2), 0.0)
        pair = layer + one
        tops = carry + (inclusive - layer)
        carry = carry + (pair + turn(pair, 2))
        moved = turn(ratio, 1)
        slope = ratio - jnp.where(lane_level >= 1, moved, last)
        last = moved
        offset = offset + slope * tops
        for count in range(levels):
            tops_turned[source * levels + count] = turn(tops, count) if count else tops
            slopes_turned[source * levels + count] = turn(slope, count) if count else slope
    offset = offset + turn(offset, 1)
    offset = offset + turn(offset, 2)
    mass_cols[here, :] = carry
    targets = [carry * fraction_cols[group, here, :] for group in range(groups)]

    def accumulate(index, sums):
        tops, slope = tops_turned[index], slopes_turned[index]
        return tuple(s + slope * jnp.maximum(t, tops) for s, t in zip(sums, targets))

    sums = lax.fori_loop(0, sources * levels, accumulate, (zero,) * groups, unroll=4)
    for group in range(groups):
        below[group, here, :] = sums[group] - offset


def peers_of(n_lev, ring):
    lev = lax.axis_index("lev")
    planes = n_lev // ring
    hops = sorted(range(ring), key=lambda hop: -min(hop, ring - hop))
    return [
        lax.rem(lev // ring + plane, planes) * ring + lax.rem(lax.rem(lev, ring) + hop, ring)
        for hop in hops for plane in range(planes) if (plane, hop) != (0, 0)
    ]


def send(peers, source, target, sent, got, which, first, count):
    started = []
    lev = lax.axis_index("lev")
    for index, other in enumerate(peers):
        copy = pltpu.make_async_remote_copy(
            src_ref=source.at[other, pl.ds(first, count)], dst_ref=target.at[lev, pl.ds(first, count)],
            send_sem=sent.at[which, index], recv_sem=got.at[which, index],
            device_id={"lev": other}, device_id_type=MESH,
        )
        copy.start()
        started.append(copy)
    return started


def add_filter(cut_in, tend_rows, tend_cols, cut_lanes, tables, tracer):
    rows = cut_in.shape[1]
    to_columns(tend_rows, tend_cols)
    cut = spread_lanes(cut_in[...].astype(jnp.float32))
    for level in range(LANES // rows):
        cut_lanes[:, pl.ds(level * rows, rows)] = jnp.broadcast_to(cut, (8, rows))
    add_damped(cut_lanes[pl.ds(0, 1), :], tend_cols, tables, tracer)


def spread_lanes(values):
    return jnp.concatenate([values[:, 8:], values[:, :8]], axis=1)


def is_polar(n_lat):
    lat = lax.axis_index("lat")
    return (lat < 2) | (lat >= n_lat - 2)


def choose(columns, target, rows, part):
    n_lev, count, _ = target.shape
    dest = columns.shape[0] // n_lev
    pairs = dest // 16

    @pl.loop(0, n_lev)
    def _(other):
        for pair in range(pairs):
            start = other * dest + 16 * pair
            first = columns[pl.ds(pl.multiple_of(start, 8), 8), :]
            second = columns[pl.ds(pl.multiple_of(start + 8, 8), 8), :]
            target[other, pl.ds(8 * pair, 8), :] = pair_up(first, second, rows)[part]
        if count > 8 * pairs:
            target[other, pl.ds(8 * pairs, 8), :] = columns[pl.ds(pl.multiple_of(other * dest + 16 * pairs, 8), 8), :]


def step_kernel(
    n_lat, n_lev, ring, lat_total, chunks,
    thick_hbm, tracer_hbm, lon_hbm, lat_hbm, cut_hbm, weights_hbm, tables_hbm,
    below, fraction, mass_cols,
    cut_in, weights_in, tables, thick_in, tracer_in, lon_in, lat_in,
    thick_rows, tracer_rows, tend_rows, to_north, to_south, south_rows, north_rows, third, inner_first,
    columns, tend_cols, cut_lanes, thick_middle_send, tracer_middle_send, thick_middle, tracer_middle,
    thick_send, tracer_send, thick_cols, tracer_cols, fraction_cols, tops_turned, slopes_turned,
    load_sem, other_sem, ready, halo_sent, halo_got, middle_sent, middle_got, sent, got,
):
    levels, rows, _ = thick_in.shape
    middle, outer = thick_middle.shape[1], thick_cols.shape[1]
    lat, lev = lax.axis_index("lat"), lax.axis_index("lev")
    polar = is_polar(n_lat)
    odd = lax.rem(lat, 2)
    north, south = lax.rem(lat + 1, n_lat), lax.rem(lat + n_lat - 1, n_lat)
    peers = peers_of(n_lev, ring)
    barrier = pltpu.get_barrier_semaphore()
    for other in peers:
        pl.semaphore_signal(barrier, inc=1, device_id={"lev": other}, device_id_type=MESH)

    @pl.when(odd == 0)
    def _():
        for place in (north, south):
            pl.semaphore_signal(barrier, inc=1, device_id={"lat": place}, device_id_type=MESH)

    inputs = ((thick_hbm, thick_in), (tracer_hbm, tracer_in), (lat_hbm, lat_in), (lon_hbm, lon_in))

    def load(level):
        return [
            pltpu.make_async_copy(source.at[level], target.at[level], load_sem.at[level, i])
            for i, (source, target) in enumerate(inputs)
        ]

    def arrive(level):
        for copy in load(level):
            copy.wait()

    others = [
        pltpu.make_async_copy(source, target, other_sem.at[i])
        for i, (source, target) in enumerate(((weights_hbm, weights_in), (cut_hbm, cut_in), (tables_hbm, tables)))
    ]
    for level in range(levels):
        for copy in load(level):
            copy.start()
    for copy in others[:2]:
        copy.start()

    @pl.when(polar)
    def _():
        others[2].start()

    inner_rows(
        lat_total, (thick_in, tracer_in, lat_in, lon_in), arrive,
        thick_rows, tracer_rows, tend_rows, to_north, to_south, third, inner_first,
    )

    @pl.when(odd == 0)
    def _():
        pl.semaphore_wait(barrier, len(peers))

    @pl.when(odd == 1)
    def _():
        pl.semaphore_wait(barrier, len(peers) + 2)

    halos = [
        pltpu.make_async_remote_copy(
            src_ref=source, dst_ref=target, send_sem=halo_sent.at[side], recv_sem=halo_got.at[side],
            device_id={"lat": place}, device_id_type=MESH,
        )
        for side, (source, target, place) in enumerate(((to_north, south_rows, north), (to_south, north_rows, south)))
    ]

    @pl.when(odd == 1)
    def _():
        for side, place in enumerate((north, south)):
            pl.semaphore_signal(ready.at[side], inc=1, device_id={"lat": place}, device_id_type=MESH)
        for copy in halos:
            copy.start()

    to_columns(thick_rows, columns)
    choose(columns, thick_middle_send, rows, 0)
    thick_moving = send(peers, thick_middle_send, thick_middle, middle_sent, middle_got, 0, 0, middle)

    @pl.when(odd == 0)
    def _():
        for side in range(2):
            pl.semaphore_wait(ready.at[side], 1)
        for copy in halos:
            copy.start()

    to_columns(tracer_rows, columns)
    for copy in others[:2]:
        copy.wait()

    @pl.when(polar)
    def _():
        others[2].wait()
        add_filter(cut_in, tend_rows, tend_cols, cut_lanes, tables, columns)

    choose(columns, tracer_middle_send, rows, 0)
    tracer_moving = send(peers, tracer_middle_send, tracer_middle, middle_sent, middle_got, 1, 0, middle)
    thick_middle[lev] = thick_middle_send[lev]
    tracer_middle[lev] = tracer_middle_send[lev]
    for copy in halos:
        copy.wait()
    edges(
        lat_total, rows, south_rows, north_rows, to_north, to_south, third, inner_first, thick_rows, tracer_rows, tend_rows
    )
    to_columns(thick_rows, columns)
    choose(columns, thick_send, rows, 1)
    thick_copies = send(peers, thick_send, thick_cols, sent, got, 0, 0, outer)
    to_columns(tracer_rows, columns)

    @pl.when(polar)
    def _():
        add_filter(cut_in, tend_rows, tend_cols, cut_lanes, tables, columns)

    choose(columns, tracer_send, rows, 1)
    bounds = [sum(chunks[:i]) for i in range(len(chunks) + 1)]
    tracer_copies = [
        send(peers, tracer_send, tracer_cols, sent, got, 1 + i, 8 * bounds[i], 8 * chunks[i]) for i in range(len(chunks))
    ]
    thick_cols[lev] = thick_send[lev]
    tracer_cols[lev] = tracer_send[lev]
    prepare_weights(weights_in, fraction, fraction_cols)
    for copy in thick_moving + tracer_moving:
        copy.wait()

    @pl.loop(0, middle // 8)
    def _(piece):
        interpolate(
            rows, piece, piece, thick_middle, tracer_middle, fraction_cols, tops_turned, slopes_turned, below, mass_cols
        )

    for copy in thick_copies:
        copy.wait()
    for i in range(len(chunks)):
        for copy in tracer_copies[i]:
            copy.wait()

        @pl.loop(bounds[i], bounds[i + 1])
        def _(piece):
            interpolate(
                rows, piece, middle // 8 + piece, thick_cols, tracer_cols, fraction_cols, tops_turned, slopes_turned,
                below, mass_cols,
            )


def finish_kernel(below, fraction, mass_cols, thick_hbm, tracer_hbm, new_thick, new_tracer, sorted_cols, sems):
    groups = below.shape[0]
    levels, rows, dest = new_thick.shape[0] // groups, new_thick.shape[1], new_thick.shape[2]
    pieces = dest // 8
    low = lane_half(rows)

    def to_rows(source, slot):
        for pair in range(pieces // 2):
            middle = source[8 * pair : 8 * pair + 8]
            outer = source[8 * (pieces // 2 + pair) : 8 * (pieces // 2 + pair) + 8]
            sorted_cols[slot, pl.ds(16 * pair, 8), :] = jnp.where(low, middle, pltpu.roll(outer, rows // 2, axis=1))
            sorted_cols[slot, pl.ds(16 * pair + 8, 8), :] = jnp.where(low, pltpu.roll(middle, LANES - rows // 2, axis=1), outer)
        if pieces % 2:
            sorted_cols[slot, pl.ds(dest - 8, 8), :] = source[dest - 8 : dest]
        turned = sorted_cols[slot].T.reshape(levels, rows, LANES)
        return jnp.concatenate([turned[:, rows - 8 :], turned[:, : rows - 8]], axis=1)

    mass = to_rows(mass_cols[...], groups)[0, :, :dest]
    target_before = below_before = jnp.zeros((rows, dest), jnp.float32)
    copies = []

    def put(which, group, source, target):
        place = pl.ds(group * levels, levels)
        copy = pltpu.make_async_copy(source.at[place], target.at[place], sems.at[which, group])
        copy.start()
        copies.append(copy)

    for group in range(groups):
        block = to_rows(below[group], group)
        for inner in range(levels):
            level = group * levels + inner
            target = mass * fraction[level, :, pl.ds(0, dest)]
            new_thick[level] = target - target_before
            target_before = target
            now = block[inner, :, :dest]
            new_tracer[level] = now - below_before
            below_before = now
        put(0, group, new_thick, thick_hbm)
        put(1, group, new_tracer, tracer_hbm)
    for copy in copies:
        copy.wait()


def on_device(n_lat, n_lev, thickness, tracer_mass, courant_lon, courant_lat, filter_cut, target_weights):
    levels, rows, width = thickness.shape
    lat_total = n_lat * rows
    dest = width // n_lev
    level_total = target_weights.shape[0]
    groups = level_total * rows // LANES
    tables = jnp.asarray(fourier_tables(width))
    ring = min(n_lev, 8)
    pieces = dest // 8
    middle, outer = 8 * (pieces // 2), 8 * (pieces - pieces // 2)
    last = pieces - pieces // 2
    chunks = (last - last // 2 - 1, last // 2, 1)
    vmem, hbm = pl.BlockSpec(memory_space=pltpu.VMEM), pl.BlockSpec(memory_space=pltpu.HBM)
    f32, dma = jnp.float32, pltpu.SemaphoreType.DMA

    def in_hbm(*arrays):
        return [pltpu.with_memory_space_constraint(array, pltpu.HBM) for array in arrays]

    def scratch(kind, *shapes):
        return [pltpu.VMEM(shape, kind) for shape in shapes]

    def outs(*shapes):
        return tuple(jax.ShapeDtypeStruct(shape, f32) for shape in shapes)

    band = (LANES, width)
    pack = (4, 2 * levels, width)
    below, fraction, mass_cols = pl.pallas_call(
        functools.partial(step_kernel, n_lat, n_lev, ring, lat_total, chunks),
        out_shape=outs((groups, dest, LANES), (level_total, rows, LANES), (dest, LANES)),
        in_specs=[hbm] * 7,
        out_specs=(vmem,) * 3,
        scratch_shapes=scratch(jnp.int32, (1, rows), target_weights.shape)
        + scratch(jnp.bfloat16, tables.shape)
        + scratch(
            f32, *[thickness.shape] * 4, band, band, band, *[pack] * 5, (2, 2 * levels, width),
            (width, LANES), (width, LANES), (8, LANES),
            *[(n_lev, middle, LANES)] * 4, *[(n_lev, outer, LANES)] * 4, (groups, dest, LANES), *[(level_total, 8, LANES)] * 2,
        )
        + [dma((levels, 4)), dma((3,)), pltpu.SemaphoreType.REGULAR((2,)), dma((2,)), dma((2,))]
        + [dma((2, n_lev - 1))] * 2 + [dma((1 + len(chunks), n_lev - 1))] * 2,
        compiler_params=pltpu.CompilerParams(collective_id=0, has_side_effects=True, vmem_limit_bytes=32 << 20),
        name="step",
    )(*in_hbm(thickness, tracer_mass, courant_lon, courant_lat, filter_cut.reshape(1, rows), target_weights, tables))
    result = jax.ShapeDtypeStruct(target_weights.shape, f32)
    return pl.pallas_call(
        finish_kernel,
        out_shape=(result, result),
        in_specs=[vmem] * 3,
        out_specs=(hbm, hbm),
        scratch_shapes=scratch(f32, target_weights.shape, target_weights.shape, (groups + 1, LANES, LANES))
        + [dma((2, groups))],
        compiler_params=pltpu.CompilerParams(vmem_limit_bytes=16 << 20),
        name="finish",
    )(below, fraction, mass_cols)


def solution(mesh):
    n_lat, n_lev = mesh.shape["lat"], mesh.shape["lev"]
    placed = (
        P("lev", "lat", None),
        P("lev", "lat", None),
        P("lev", "lat", None),
        P("lev", "lat", None),
        P("lat"),
        P(None, "lat", "lev"),
    )
    return jax.shard_map(
        functools.partial(on_device, n_lat, n_lev),
        mesh=mesh,
        in_specs=placed,
        out_specs=(P(None, "lat", "lev"), P(None, "lat", "lev")),
        check_vma=False,
    )
```

time: 52.7 us -> 47.7 us (0.905)
  the two profiles are of different devices: /device:TPU:6 before, /device:TPU:8 now
where the time goes in v1:
time: 47.7 us; the launch traced here: 47.5 us
  Pallas kernels  46.9 us (98%)
  between operations  0.64 us (1%)
    pallas_call x1, Pallas kernels, on_device(): pl.pallas_call(functools.partial(step_kernel, n_lat, n_lev, ring, lat_tot...  45.1 us
    pallas_call x1, Pallas kernels, on_device(): pl.pallas_call(finish_kernel, out_shape=(result, result), in_specs=[vmem]...  1.82 us

profile of v1, /device:TPU:8, one launch (start us, length us, event | category | flops | bytes accessed | tf_op | source)
XLA Modules:
  0.0 47.5 jit_solution(3620986980531113350)
XLA Ops:
  0.6 45.1 %step.1 = (f32[16,72,128]{2,1,0:T(8,128)S(1)}, f32[64,32,128]{2,1,0:T(8,128)S(1)}, f32[72,128]{1,0:T(8,128)S(1)}) custom-call(f32[4,32,1152]{2,1,0:T(8,128)} %thick_hbm.1, f32[4,32,1152]{2,1,0:T(8,128)} %tracer_hbm.1, f32[4,32,1152]{2,1,0:T(8,128)} %lon_hbm.1, f32[4,32,1152]{2,1,0:T(8,128)} %lat_hbm.1, s32[1,32]{1,0:T(1,128)} %bitcast.1, ...), custom_call_target="tpu_custom_call" | custom-call | tf_op jit(solution)/shard_map/step/pallas_call | solution.py:547
  45.7 1.8 %finish.1 = (f32[64,32,72]{2,1,0:T(8,128)}, f32[64,32,72]{2,1,0:T(8,128)}) custom-call(f32[16,72,128]{2,1,0:T(8,128)S(1)} %get-tuple-element.5.below, f32[64,32,128]{2,1,0:T(8,128)S(1)} %get-tuple-element.6.fraction, f32[72,128]{1,0:T(8,128)S(1)} %get-tuple-element.7.mass_cols), custom_call_target="tpu_custom_call" | custom-call | tf_op jit(solution)/shard_map/finish/pallas_call | solution.py:565
